TPU v7x, 512 devices: a whole 4x4x16 slice. The times are simulated.
512 devices in a mesh: chan: 64 (over y_lo, z, core), loc: 8 (over y_hi, x).
Axes of the slice: x: 4, y: 4 (y_hi: 2, y_lo: 2; y = y_hi * 2 + y_lo), z: 16, core: 2. Of those that a mesh axis runs over, the one named last changes fastest.
Arguments:
- pixels: bfloat16 [2048, 256, 256], P('loc', 'chan'), may hold values from -6 to 6
- patch_mask: int32 [2048, 256], P('loc', 'chan'), may hold values 0 or 1
- group_map: int32 [256], replicated, may hold values from 0 to 63, as said below
- embed_weight: bfloat16 [256, 2048], P(None, 'loc'), may hold values from -0.375 to 0.375
- mask_token: bfloat16 [2048], replicated, may hold values from -6 to 6
- chan_embed: bfloat16 [256, 2048], P('chan'), may hold values from -3 to 3
- agg_weight: float32 [256], P('chan'), may hold values from 0.5 to 2
- query_key: bfloat16 [16, 2048], replicated, may hold values from -0.02734375 to 0.02734375
- group_bias: float32 [16, 64], replicated, may hold values from -0.5 to 255
- norm_gain: float32 [2048], replicated, may hold values from 0.25 to 1.75
- head_weight: bfloat16 [2048, 256, 256], P(None, 'chan'), may hold values from -0.125 to 0.125
- head_bias: float32 [256, 256], P('chan'), may hold values from -3 to 3
Outputs:
- rebuilt: bfloat16 [2048, 256, 256], P('loc', 'chan')
Inputs may be any that keep to these rules, and one draw needn't show every extreme that they name: `group_map`: the 4 channels of each bundle (channels k * 4 to k * 4 + 3) name at most two distinct groups.
All inputs are finite; a program needn't handle non-finite values. No bound on the sum of `patch_mask` on one device may be relied on, other than what follows from the above.
Results may differ from a plain program's by a relative error of at most 0.0051.
Values may be sent and summed in bfloat16 or wider, within the bound.
A program may use at most 64 MiB of HBM per device.

v0:
```python
import math
import jax
import jax.numpy as jnp
from jax import lax
from jax.sharding import PartitionSpec as P

C = 256
E = 2048
G = 64
H = 16
BUNDLE = 4


def shards(
    pixels,
    patch_mask,
    group_map,
    embed_weight,
    mask_token,
    chan_embed,
    agg_weight,
    query_key,
    group_bias,
    norm_gain,
    head_weight,
    head_bias,
):
    locs, own_channels, pixel_count = pixels.shape
    peers = lax.axis_size("chan")
    bundled = group_map.reshape(C // BUNDLE, BUNDLE)
    lowest = jnp.min(bundled, axis=1)
    highest = jnp.max(bundled, axis=1)
    slot_group = jnp.stack([lowest, highest], axis=1)
    me = lax.axis_index("chan")
    own = lax.dynamic_slice_in_dim(bundled, me, 1, 0)[0]
    own_slot = (own != jnp.min(own)).astype(jnp.int32)
    choose = own_slot[None, :] == jnp.arange(2)[:, None]
    loc_peers = lax.axis_size("loc")
    copies = lax.all_to_all(
        jnp.broadcast_to(embed_weight[None], (loc_peers, *embed_weight.shape)),
        "loc",
        0,
        0,
        tiled=True,
    )
    weight = jnp.moveaxis(copies, 0, 1).reshape(pixel_count, E)
    projected = jnp.dot(
        pixels.reshape(locs * own_channels, pixel_count), weight, preferred_element_type=jnp.float32
    ).reshape(locs, own_channels, E)
    hidden = (patch_mask == 1)[:, :, None]
    pre = jnp.where(hidden, mask_token.astype(jnp.float32)[None, None], projected)
    pre = pre + chan_embed.astype(jnp.float32)[None]
    weighted = (
        pre * (1.0 + lax.erf(pre * (1.0 / math.sqrt(2.0)))) * (0.5 * agg_weight)[None, :, None]
    )
    weighted = weighted.astype(jnp.bfloat16)
    sums = jnp.einsum(
        "lke,sk->sle", weighted, choose.astype(jnp.bfloat16), preferred_element_type=jnp.float32
    ).astype(jnp.bfloat16)
    part = jnp.einsum("sle,he->slh", sums, query_key, preferred_element_type=jnp.float32)
    part = part.reshape(2, locs * H)
    every = lax.all_gather(part, "chan", axis=0, tiled=True)
    to_group = (jnp.arange(G)[:, None] == slot_group.reshape(-1)[None]).astype(jnp.float32)
    scores = jnp.dot(to_group, every, precision=lax.Precision.HIGHEST).reshape(G, locs, H)
    scores = scores + group_bias.T[:, None, :]
    attn = jax.nn.softmax(scores, axis=0)
    own_group = jnp.stack([jnp.min(own), jnp.max(own)])
    own_attn = jnp.take(attn, own_group, axis=0)
    pooled = (sums.reshape(2, locs, H, E // H) * own_attn[..., None]).sum(0).reshape(locs, E)
    pooled = lax.psum_scatter(pooled, "chan", scatter_dimension=0, tiled=True)
    inverse = lax.rsqrt(jnp.mean(pooled * pooled, axis=-1, keepdims=True) + 1e-06)
    joined = (pooled * inverse * norm_gain[None]).astype(jnp.bfloat16)
    joined = lax.all_gather(joined, "chan", axis=0, tiled=True)
    decoded = jnp.dot(
        joined,
        head_weight.reshape(E, own_channels * pixel_count),
        preferred_element_type=jnp.float32,
    )
    decoded = decoded + head_bias.reshape(1, own_channels * pixel_count)
    return decoded.astype(jnp.bfloat16).reshape(locs, own_channels, pixel_count)


def solution(mesh):
    return jax.shard_map(
        shards,
        mesh=mesh,
        in_specs=(
            P("loc", "chan", None),
            P("loc", "chan"),
            P(),
            P(None, "loc"),
            P(),
            P("chan", None),
            P("chan"),
            P(),
            P(),
            P(),
            P(None, "chan", None),
            P("chan", None),
        ),
        out_specs=P("loc", "chan", None),
        check_vma=False,
    )
```

profile of v0, /device:TPU:1, one launch (start us, length us, event | category | flops | bytes accessed | tf_op | source)
XLA Modules:
  0.0 764.5 jit_solution(2735376849102494480)
XLA Ops:
  6.5 2.0 broadcast_in_dim.27
  8.6 7.5 all-to-all-start
  16.1 0.8 reshape.155
  16.9 0.7 convert_element_type.27
  17.6 0.7 convert_element_type.26
  18.3 0.7 fusion.19
  19.0 0.6 fusion.16
  19.6 0.7 broadcast_multiply_fusion
  20.2 0.7 broadcast_compare_fusion
  20.9 12.3 %all-to-all-done = bf16[8,256,256]{2,1,0:T(8,128)(2,1)S(1)} async-done(((bf16[8,256,256]{2,1,0:T(8,128)(2,1)}), bf16[8,256,256]{2,1,0:T(8,128)(2,1)S(1)}, u32[]{:S(2)}, u32[]{:S(2)}) %all-to-all-start) | async-done | bytes 1048608 | tf_op jit(solution)/shard_map/all_to_all | solution.py:39
  33.3 0.6 copy.40
  33.9 0.5 reshape.175
  34.4 3.0 multiply_convert_fusion
  37.4 3.0 fusion.2
  40.5 1.4 copy-done.1
  41.8 1.2 fusion.5
  43.1 0.8 reshape.170
  43.9 0.1 fusion.21
  44.0 0.1 copy.43
  44.1 0.1 eq.47
  44.4 0.1 add.72.clone
  44.5 0.6 copy.50
  45.1 1.3 fusion.17
  46.4 1.3 compare_and_fusion
  47.7 119.1 %all-gather.5.cloned.1.call-done = f32[64,2,4096]{2,1,0:T(2,128)} async-done(((f32[1,2,4096]{2,1,0:T(2,128)}), f32[64,2,4096]{2,1,0:T(2,128)}) %all-gather.5.cloned.1.call-update) | async-done | bytes 2097168 | tf_op jit(solution)/shard_map/all_gather | solution.py:62
  166.8 2.7 reshape.171
  169.5 2.4 fusion.22
  171.9 0.1 sub.15
  172.0 1.4 exponential_reduce_fusion
  173.4 0.1 div.13
  173.6 1.8 copy.46
  175.5 1.4 copy.48
  176.9 0.2 exponential_divide_fusion
  177.2 0.6 gather_fusion
  177.8 0.2 copy.53
  178.0 2.6 mul.56
  180.6 5.9 mul.57
  186.5 10.0 %multiply_reduce_fusion = f32[256,2048]{1,0:T(8,128)} fusion(f32[2,256,2048]{2,0,1:T(2,128)} %mul.57, bf16[2,256,2048]{2,0,1:T(2,128)(2,1)S(1)} %copy-done.2), kind=kLoop, calls=%fused_computation.2 | loop fusion | flops 2621440 | bytes 8388608 | tf_op jit(solution)/shard_map/reduce_sum | solution.py:69
  196.5 0.3 all-gather.7.cloned.1.call-start
  196.8 1.3 dynamic-slice
  198.7 435.7 %all-reduce.3.cloned.1.call-done = f32[256,2048]{1,0:T(8,128)} async-done(((f32[256,2048]{1,0:T(8,128)}), f32[256,2048]{1,0:T(8,128)}) %all-reduce.3.cloned.1.call-update) | async-done | bytes 2097168
  634.4 1.0 multiply_reduce_fusion.1
  635.4 1.5 fusion.11
  637.0 5.2 copy.56
  642.2 109.9 %all-gather.7.cloned.1.call-done = bf16[64,4,2048]{2,1,0:T(4,128)(2,1)} async-done(((bf16[1,4,2048]{2,1,0:T(4,128)(2,1)}), bf16[64,4,2048]{2,1,0:T(4,128)(2,1)}) %all-gather.7.cloned.1.call-update) | async-done | bytes 1048592 | tf_op jit(solution)/shard_map/all_gather | solution.py:73
  752.1 1.3 reshape.173
  753.4 3.4 fusion.7
  756.8 1.2 reshape.160
  (26 shorter events, 0.5 us)
Async XLA Ops:
  6.5 35.3 %copy-start = (bf16[16,2048]{1,0:T(8,128)(2,1)S(1)}, bf16[16,2048]{1,0:T(8,128)(2,1)}, u32[]{:S(2)}) copy-start(bf16[16,2048]{1,0:T(8,128)(2,1)} %param.19) | copy-start | bytes 196612
  6.5 27.9 %copy-start.6 = (bf16[256,4,256]{2,1,0:T(4,128)(2,1)S(1)}, bf16[256,4,256]{2,1,0:T(4,128)(2,1)}, u32[]{:S(2)}) copy-start(bf16[256,4,256]{2,1,0:T(4,128)(2,1)} %param.12) | copy-start | bytes 1572868
  8.6 24.7 %all-to-all-start = ((bf16[8,256,256]{2,1,0:T(8,128)(2,1)}), bf16[8,256,256]{2,1,0:T(8,128)(2,1)S(1)}, u32[]{:S(2)}, u32[]{:S(2)}) async-start(bf16[8,256,256]{2,1,0:T(8,128)(2,1)} %broadcast_in_dim.27), calls=%async_computation | async-start | bytes 2097152 | tf_op jit(solution)/shard_map/all_to_all | solution.py:39
  16.0 150.8 %all-gather.5.cloned.1.call-start = ((), (), s32[]{:S(2)}) async-start(), calls=%async_computation.1 | async-start | bytes 2129920 | tf_op jit(solution)/shard_map/all_gather | solution.py:62
  37.4 6.9 copy-start.3
  40.4 1.4 copy-start.1
  43.9 590.6 %all-reduce.3.cloned.1.call-start = ((), (), s32[]{:S(2)}) async-start(), calls=%async_computation.3 | async-start | bytes 4194304
  180.6 5.9 copy-start.2
  186.5 448.9 %copy-start.4 = (f32[2048]{0:T(1024)S(1)}, f32[2048]{0:T(1024)}, u32[]{:S(2)}) copy-start(f32[2048]{0:T(1024)} %param.21) | copy-start | bytes 24580
  196.5 555.5 %all-gather.7.cloned.1.call-start = ((), (), s32[]{:S(2)}) async-start(), calls=%async_computation.2 | async-start | bytes 1064960 | tf_op jit(solution)/shard_map/all_gather | solution.py:73
  637.0 5.2 copy-start.5
Sparse Core Ops, SparseCore 0:
  44.0 122.8 all-gather.4
  196.7 437.7 all-reduce.2
  637.1 114.9 all-gather.6
where the time goes:
time: 765 us
  waiting for transfers between devices  677 us (88%)
  local copies, waits for them, and re-layouts  31.6 us (4%)
  other arithmetic  21 us (3%)
  between operations  14 us (2%)
  matrix products  13 us (2%)
  starting transfers between devices  7.81 us (1%)
    unnamed x4, waiting for transfers between devices  436 us
    all_gather x1, waiting for transfers between devices, shards(): every = lax.all_gather(part, 'chan', axis=0, tiled=True)  119 us
    all_gather x1, waiting for transfers between devices, shards(): joined = lax.all_gather(joined, 'chan', axis=0, tiled=True)  110 us
  transfers between devices with their start and end apart: 4, of which 4 were waited for; matrix products, arithmetic and copies ran while one was open for 2% of the time, Pallas kernels for 0%

commit v1 on v0

--- a/solution.py
+++ b/solution.py
@@ -70,7 +70,9 @@
     pooled = lax.psum_scatter(pooled, "chan", scatter_dimension=0, tiled=True)
     inverse = lax.rsqrt(jnp.mean(pooled * pooled, axis=-1, keepdims=True) + 1e-06)
     joined = (pooled * inverse * norm_gain[None]).astype(jnp.bfloat16)
-    joined = lax.all_gather(joined, "chan", axis=0, tiled=True)
+    joined = jnp.concatenate(
+        lax.all_to_all(jnp.stack([joined] * lax.axis_size("chan")), "chan", 0, 0), axis=0
+    )
     decoded = jnp.dot(
         joined,
         head_weight.reshape(E, own_channels * pixel_count),

time: 765 us -> 710 us (0.928)
  waiting for transfers between devices: 677 us -> 613 us
    all_gather x1 -> x0, waiting for transfers between devices: 110 us -> none  [shards(): joined = lax.all_gather(joined, 'chan', axis=0, tiled=True)]
    all_to_all x0 -> x1, waiting for transfers between devices: none -> 45.1 us  [shards(): lax.all_to_all(jnp.stack([joined] * lax.axis_size('chan')), 'chan', 0, 0)]
    unnamed x4 -> x3, waiting for transfers between devices: 436 us -> 436 us
where the time goes in v1:
time: 710 us; the launch traced here: 706 us
  waiting for transfers between devices  613 us (86%)
  local copies, waits for them, and re-layouts  32 us (5%)
  other arithmetic  20.4 us (3%)
  between operations  14.3 us (2%)
  starting transfers between devices  13.9 us (2%)
  matrix products  13 us (2%)
    unnamed x3, waiting for transfers between devices  436 us
    all_gather x1, waiting for transfers between devices, shards(): every = lax.all_gather(part, 'chan', axis=0, tiled=True)  119 us
    all_to_all x1, waiting for transfers between devices, shards(): lax.all_to_all(jnp.stack([joined] * lax.axis_size('chan')), 'chan', 0, 0)  45.1 us
  transfers between devices with their start and end apart: 4, of which 4 were waited for; matrix products, arithmetic and copies ran while one was open for 2% of the time, Pallas kernels for 0%

profile of v1, /device:TPU:1, one launch (start us, length us, event | category | flops | bytes accessed | tf_op | source)
XLA Modules:
  0.0 706.2 jit_solution(5124682912213723581)
XLA Ops:
  6.5 2.0 broadcast_in_dim.27
  8.6 7.5 %all-to-all-start = ((bf16[8,256,256]{2,1,0:T(8,128)(2,1)}), bf16[8,256,256]{2,1,0:T(8,128)(2,1)S(1)}, u32[]{:S(2)}, u32[]{:S(2)}) async-start(bf16[8,256,256]{2,1,0:T(8,128)(2,1)} %broadcast_in_dim.27), calls=%async_computation | async-start | bytes 2097152 | tf_op jit(solution)/shard_map/all_to_all | solution.py:39
  16.1 0.8 reshape.160
  16.9 0.7 convert_element_type.27
  17.6 0.7 convert_element_type.26
  18.3 0.7 fusion.18
  19.0 0.6 fusion.15
  19.6 0.7 broadcast_multiply_fusion
  20.2 0.7 broadcast_compare_fusion
  20.9 12.3 %all-to-all-done = bf16[8,256,256]{2,1,0:T(8,128)(2,1)S(1)} async-done(((bf16[8,256,256]{2,1,0:T(8,128)(2,1)}), bf16[8,256,256]{2,1,0:T(8,128)(2,1)S(1)}, u32[]{:S(2)}, u32[]{:S(2)}) %all-to-all-start) | async-done | bytes 1048608 | tf_op jit(solution)/shard_map/all_to_all | solution.py:39
  33.3 0.6 copy.40
  33.9 0.5 reshape.179
  34.4 3.0 multiply_convert_fusion
  37.4 3.0 fusion.2
  40.5 1.4 copy-done.1
  41.8 1.2 fusion.5
  43.1 0.8 reshape.176
  43.9 0.1 fusion.20
  44.0 0.1 copy.43
  44.1 0.1 eq.47
  44.4 0.1 add.72.clone
  44.5 0.6 copy.50
  45.1 1.3 fusion.16
  46.4 1.3 compare_and_fusion
  47.7 119.1 %all-gather.3.cloned.1.call-done = f32[64,2,4096]{2,1,0:T(2,128)} async-done(((f32[1,2,4096]{2,1,0:T(2,128)}), f32[64,2,4096]{2,1,0:T(2,128)}) %all-gather.3.cloned.1.call-update) | async-done | bytes 2097168 | tf_op jit(solution)/shard_map/all_gather | solution.py:62
  166.8 2.7 reshape.177
  169.5 2.3 fusion.21
  172.0 1.4 exponential_reduce_fusion
  173.4 0.1 div.13
  173.6 1.8 copy.46
  175.5 1.4 copy.48
  176.9 0.2 exponential_divide_fusion
  177.2 0.6 gather_fusion
  177.8 0.2 copy.53
  178.0 2.6 mul.56
  180.6 5.9 mul.57
  186.5 10.0 %multiply_reduce_fusion = f32[256,2048]{1,0:T(8,128)} fusion(f32[2,256,2048]{2,0,1:T(2,128)} %mul.57, bf16[2,256,2048]{2,0,1:T(2,128)(2,1)S(1)} %copy-done.2), kind=kLoop, calls=%fused_computation.2 | loop fusion | flops 2621440 | bytes 8388608 | tf_op jit(solution)/shard_map/reduce_sum | solution.py:69
  196.5 1.3 dynamic-slice
  198.5 436.0 %all-reduce.3.cloned.1.call-done = f32[256,2048]{1,0:T(8,128)} async-done(((f32[256,2048]{1,0:T(8,128)}), f32[256,2048]{1,0:T(8,128)}) %all-reduce.3.cloned.1.call-update) | async-done | bytes 2097168
  634.5 1.0 multiply_reduce_fusion.1
  635.5 0.9 multiply_convert_fusion.1
  636.4 1.5 stack.29
  637.9 6.3 all-to-all-start.1
  644.2 5.2 copy.56
  649.4 45.1 %all-to-all-done.1 = bf16[64,4,2048]{2,1,0:T(4,128)(2,1)S(1)} async-done(((bf16[64,4,2048]{2,1,0:T(4,128)(2,1)}), bf16[64,4,2048]{2,1,0:T(4,128)(2,1)S(1)}, u32[]{:S(2)}, u32[]{:S(2)}) %all-to-all-start.1) | async-done | bytes 1048608 | tf_op jit(solution)/shard_map/all_to_all | solution.py:74
  694.5 0.3 reshape.164
  694.8 3.4 fusion.7
  698.2 1.2 reshape.166
  (26 shorter events, 0.5 us)
Async XLA Ops:
  6.5 35.3 %copy-start = (bf16[16,2048]{1,0:T(8,128)(2,1)S(1)}, bf16[16,2048]{1,0:T(8,128)(2,1)}, u32[]{:S(2)}) copy-start(bf16[16,2048]{1,0:T(8,128)(2,1)} %param.19) | copy-start | bytes 196612
  6.5 27.9 %copy-start.6 = (bf16[256,4,256]{2,1,0:T(4,128)(2,1)S(1)}, bf16[256,4,256]{2,1,0:T(4,128)(2,1)}, u32[]{:S(2)}) copy-start(bf16[256,4,256]{2,1,0:T(4,128)(2,1)} %param.12) | copy-start | bytes 1572868
  8.6 24.7 %all-to-all-start = ((bf16[8,256,256]{2,1,0:T(8,128)(2,1)}), bf16[8,256,256]{2,1,0:T(8,128)(2,1)S(1)}, u32[]{:S(2)}, u32[]{:S(2)}) async-start(bf16[8,256,256]{2,1,0:T(8,128)(2,1)} %broadcast_in_dim.27), calls=%async_computation | async-start | bytes 2097152 | tf_op jit(solution)/shard_map/all_to_all | solution.py:39
  16.0 150.8 %all-gather.3.cloned.1.call-start = ((), (), s32[]{:S(2)}) async-start(), calls=%async_computation.2 | async-start | bytes 2129920 | tf_op jit(solution)/shard_map/all_gather | solution.py:62
  37.4 6.9 copy-start.3
  40.4 1.4 copy-start.1
  43.9 590.6 %all-reduce.3.cloned.1.call-start = ((), (), s32[]{:S(2)}) async-start(), calls=%async_computation.3 | async-start | bytes 4194304
  180.6 5.9 copy-start.2
  186.5 449.0 %copy-start.4 = (f32[2048]{0:T(1024)S(1)}, f32[2048]{0:T(1024)}, u32[]{:S(2)}) copy-start(f32[2048]{0:T(1024)} %param.21) | copy-start | bytes 24580
  637.9 56.6 %all-to-all-start.1 = ((bf16[64,4,2048]{2,1,0:T(4,128)(2,1)}), bf16[64,4,2048]{2,1,0:T(4,128)(2,1)S(1)}, u32[]{:S(2)}, u32[]{:S(2)}) async-start(bf16[64,4,2048]{2,1,0:T(4,128)(2,1)} %stack.29), calls=%async_computation.1 | async-start | bytes 2097152 | tf_op jit(solution)/shard_map/all_to_all | solution.py:74
  644.2 5.2 copy-start.5
Sparse Core Ops, SparseCore 0:
  44.0 122.8 all-gather.2
  196.7 437.7 all-reduce.2
